TPU v7x, 32 devices: a whole 2x2x4 slice. The times are simulated.
32 devices in a mesh: dp: 8 (over z, x), ctx: 4 (over y, core).
Axes of the slice: x: 2, y: 2, z: 4, core: 2. Of those that a mesh axis runs over, the one named last changes fastest.
Arguments:
- states: bfloat16 [32, 1024, 960], P('dp', 'ctx'), may hold values from -6 to 6
- teacher: bfloat16 [32, 1024, 960], P('dp', 'ctx'), may hold values from -6 to 6
- validity: int32 [32, 1024], P('dp', 'ctx'), may hold values from 0 to 1, as said below
- chosen: int32 [32, 1024], P('dp', 'ctx'), may hold values from 0 to 1, as said below
- attn_pack: bfloat16 [960, 2560], P(None, ('dp', 'ctx')), may hold values from -1 to 1
- gate_up: bfloat16 [960, 5120], P(None, ('dp', 'ctx')), may hold values from -0.1875 to 0.1875
- down_proj: bfloat16 [960, 2560], P(None, ('dp', 'ctx')), may hold values from -0.125 to 0.125
- norm_gains: float32 [2, 960], replicated, may hold values from 0.25 to 1.75
- router: float32 [960], replicated, may hold values from -0.12 to 0.12
Outputs:
- states_out: bfloat16 [32, 1024, 960], P('dp', 'ctx')
- mse_loss: float32 [], replicated
- states_grad: float32 [32, 1024, 960], P('dp', 'ctx')
- attn_pack_grad: float32 [960, 2560], P(None, ('dp', 'ctx'))
- gate_up_grad: float32 [960, 5120], P(None, ('dp', 'ctx'))
- down_proj_grad: float32 [960, 2560], P(None, ('dp', 'ctx'))
- norm_gains_grad: float32 [2, 960], replicated
- router_grad: float32 [960], replicated
Inputs may be any that keep to these rules, and one draw needn't show every extreme that they name: `validity`: the first token of every sequence is valid. `chosen`: each sequence has 640 or 641 selected tokens, the first token always among them.
All inputs are finite; a program needn't handle non-finite values.
Results may differ from a plain program's by a relative error of at most 0.012.
Values may be sent and summed in bfloat16 or wider, within the bound.
No kernel may reach another device: no remote copies, remote signals or barrier semaphores. Data moves between devices by JAX's collectives and lax.ppermute only.
A program may use at most 320 MiB of HBM per device.

v0:
```python
import jax
import jax.numpy as jnp
from jax import lax
from jax.sharding import PartitionSpec as P

D = 960
HEADS = 15
KV_HEADS = 5
HEAD = 64
FF = 2560
MICRO = 2
EPS = 1e-05
THETA = 10000.0


def shortened(x):
    return jax.tree.map(lambda a: a.astype(jnp.bfloat16) if a.dtype == jnp.float32 else a, x)


def rope_tables(positions):
    half_head = HEAD // 2
    freqs = THETA ** (-(jnp.arange(half_head).astype(jnp.float32) * 2.0 / HEAD))
    angles = positions.astype(jnp.float32)[:, None] * freqs[None, :]
    return (jnp.cos(angles)[:, None, :], jnp.sin(angles)[:, None, :])


def rotate(values, cosine, sine):
    half_head = HEAD // 2
    first = values[..., :half_head]
    second = values[..., half_head:]
    return jnp.concatenate(
        [first * cosine - second * sine, second * cosine + first * sine], axis=-1
    )


def rotate_back(values, cosine, sine):
    half_head = HEAD // 2
    first = values[..., :half_head]
    second = values[..., half_head:]
    return jnp.concatenate(
        [first * cosine + second * sine, second * cosine - first * sine], axis=-1
    )


def norm_back(grad_out, values, inv_rms, gain_row):
    scaled = grad_out * gain_row
    return inv_rms * scaled - values * inv_rms**3 * jnp.mean(
        scaled * values, axis=-1, keepdims=True
    )


def scores_of(queries, keys, allowed):
    scores = (
        jnp.einsum("bqgrh,bkgh->bgrqk", queries, keys, preferred_element_type=jnp.float32) * 0.125
    )
    return jnp.where(allowed, scores, -jnp.inf)


def over_rows(left, right):
    return lax.dot_general(
        left, right, (((0, 1), (0, 1)), ((), ())), preferred_element_type=jnp.float32
    )


def by_columns(left, right):
    return lax.dot_general(
        left, right, (((2,), (1,)), ((), ())), preferred_element_type=jnp.float32
    )


def on_device(states, teacher, validity, chosen, attn_pack, gate_up, down_proj, norm_gains, router):
    seq_count, block_rows, width = states.shape
    seq_micro = seq_count // MICRO
    ctx_count = lax.axis_size("ctx")
    dp_count = lax.axis_size("dp")
    ctx_spot = lax.axis_index("ctx")
    seq_length = block_rows * ctx_count
    qkv_cols = D + 2 * KV_HEADS * HEAD
    kv_width = KV_HEADS * HEAD
    per_kv = HEADS // KV_HEADS
    cosine, sine = rope_tables(ctx_spot * block_rows + jnp.arange(block_rows))
    early_block = jnp.arange(seq_length) // block_rows <= ctx_spot
    valid_all = validity.astype(jnp.float32)
    chosen_all = chosen.astype(jnp.float32)
    key_flags = (validity * chosen).astype(jnp.bfloat16)
    gain_one = norm_gains[0]
    gain_two = norm_gains[1]
    packs = (attn_pack, gate_up, down_proj)
    valid_total = lax.psum(jnp.sum(valid_all), ("dp", "ctx"))
    grad_attn = jnp.zeros((D, qkv_cols + D), jnp.float32)
    grad_gu = jnp.zeros((D, 2 * FF), jnp.float32)
    grad_down = jnp.zeros((D, FF), jnp.float32)
    grad_gain_one = jnp.zeros((D,), jnp.float32)
    grad_gain_two = jnp.zeros((D,), jnp.float32)
    grad_router = jnp.zeros((D,), jnp.float32)
    energy = jnp.zeros((), jnp.float32)
    out_parts = []
    input_grads = []
    for micro_index in range(MICRO):
        lower = micro_index * seq_micro
        upper = lower + seq_micro
        x_float = states[lower:upper].astype(jnp.float32)
        teacher_rows = teacher[lower:upper].astype(jnp.float32)
        valid_rows = valid_all[lower:upper]
        chosen_rows = chosen_all[lower:upper]
        fresh = (
            lax.all_gather(packs[0], ("dp", "ctx"), axis=1, tiled=True),
            lax.all_gather(packs[1], ("dp", "ctx"), axis=1, tiled=True),
            lax.all_gather(packs[2], ("dp", "ctx"), axis=1, tiled=True),
        )
        w_attn, w_gu, w_down = fresh
        inv_one = lax.rsqrt(jnp.mean(x_float * x_float, axis=-1, keepdims=True) + EPS)
        normed = (x_float * inv_one * gain_one).astype(jnp.bfloat16)
        mixed = jnp.dot(normed, w_attn[:, :qkv_cols], preferred_element_type=jnp.float32)
        queries = mixed[..., :D].reshape(seq_micro, block_rows, HEADS, HEAD)
        keys = mixed[..., D : D + kv_width].reshape(seq_micro, block_rows, KV_HEADS, HEAD)
        values_in = mixed[..., D + kv_width :].reshape(seq_micro, block_rows, KV_HEADS, HEAD)
        rot_queries = (
            rotate(queries, cosine, sine)
            .astype(jnp.bfloat16)
            .reshape(seq_micro, block_rows, KV_HEADS, per_kv, HEAD)
        )
        rot_keys = rotate(keys, cosine, sine).astype(jnp.bfloat16)
        value_low = values_in.astype(jnp.bfloat16)
        keys_all, values_all, flags_all = (
            lax.all_gather(rot_keys, "ctx", axis=1, tiled=True),
            lax.all_gather(value_low, "ctx", axis=1, tiled=True),
            lax.all_gather(key_flags[lower:upper], "ctx", axis=1, tiled=True),
        )
        allowed = (early_block[None, :] & (flags_all > 0.5))[:, None, None, None, :]
        scores = scores_of(rot_queries, keys_all, allowed)
        row_max = jnp.max(scores, axis=-1, keepdims=True)
        expd = jnp.exp(scores - row_max)
        row_total = jnp.sum(expd, axis=-1, keepdims=True)
        log_total = row_max + jnp.log(row_total)
        probs_low = (expd / row_total).astype(jnp.bfloat16)
        heads_out = jnp.einsum(
            "bgrqk,bkgh->bqgrh", probs_low, values_all, preferred_element_type=jnp.float32
        )
        heads_low = heads_out.reshape(seq_micro, block_rows, D).astype(jnp.bfloat16)
        attn_out = by_columns(heads_low, w_attn[:, qkv_cols:])
        inner = x_float + attn_out
        inv_two = lax.rsqrt(jnp.mean(inner * inner, axis=-1, keepdims=True) + EPS)
        normed_two = (inner * inv_two * gain_two).astype(jnp.bfloat16)
        gate_both = jnp.dot(normed_two, w_gu, preferred_element_type=jnp.float32)
        gate_part = gate_both[..., :FF]
        up_part = gate_both[..., FF:]
        gate_sig = jax.nn.sigmoid(gate_part)
        hidden = (gate_part * gate_sig * up_part).astype(jnp.bfloat16)
        ffn_out = by_columns(hidden, w_down)
        gate_prob = jax.nn.sigmoid(jnp.dot(x_float, router, precision=lax.Precision.HIGHEST))
        weight_mix = chosen_rows * gate_prob
        branch = attn_out + ffn_out
        result = x_float + weight_mix[..., None] * branch
        out_parts.append(result.astype(jnp.bfloat16))
        diff = valid_rows[..., None] * (result - teacher_rows)
        energy = energy + 0.5 * jnp.sum(diff * diff)
        w_attn, w_gu, w_down = (
            lax.all_gather(packs[0], ("dp", "ctx"), axis=1, tiled=True),
            lax.all_gather(packs[1], ("dp", "ctx"), axis=1, tiled=True),
            lax.all_gather(packs[2], ("dp", "ctx"), axis=1, tiled=True),
        )
        d_branch = weight_mix[..., None] * diff
        d_logit = chosen_rows * jnp.sum(diff * branch, axis=-1) * gate_prob * (1.0 - gate_prob)
        grad_router = grad_router + jnp.einsum(
            "bt,btd->d", d_logit, x_float, precision=lax.Precision.HIGHEST
        )
        d_states = diff + d_logit[..., None] * router
        d_ffn = d_branch.astype(jnp.bfloat16)
        d_hidden = jnp.dot(d_ffn, w_down, preferred_element_type=jnp.float32)
        grad_down = grad_down + over_rows(d_ffn, hidden)
        d_gate = d_hidden * up_part * gate_sig * (1.0 + gate_part * (1.0 - gate_sig))
        d_up = d_hidden * gate_part * gate_sig
        d_gu_low = jnp.concatenate([d_gate, d_up], axis=-1).astype(jnp.bfloat16)
        d_normed_two = by_columns(d_gu_low, w_gu)
        grad_gu = grad_gu + over_rows(normed_two, d_gu_low)
        grad_gain_two = grad_gain_two + jnp.sum(d_normed_two * inner * inv_two, axis=(0, 1))
        d_inner = norm_back(d_normed_two, inner, inv_two, gain_two)
        d_states = d_states + d_inner
        d_attn_low = (d_branch + d_inner).astype(jnp.bfloat16)
        d_heads = jnp.dot(d_attn_low, w_attn[:, qkv_cols:], preferred_element_type=jnp.float32)
        d_heads_low = d_heads.astype(jnp.bfloat16).reshape(
            seq_micro, block_rows, KV_HEADS, per_kv, HEAD
        )
        grad_out_proj = over_rows(d_attn_low, heads_low)
        probs = jnp.exp(scores_of(rot_queries, keys_all, allowed) - log_total)
        d_probs = jnp.einsum(
            "bqgrh,bkgh->bgrqk", d_heads_low, values_all, preferred_element_type=jnp.float32
        )
        d_scores = (probs * (d_probs - jnp.sum(probs * d_probs, axis=-1, keepdims=True))).astype(
            jnp.bfloat16
        )
        d_queries = (
            jnp.einsum("bgrqk,bkgh->bqgrh", d_scores, keys_all, preferred_element_type=jnp.float32)
            * 0.125
        )
        d_keys_all = (
            jnp.einsum(
                "bgrqk,bqgrh->bkgh", d_scores, rot_queries, preferred_element_type=jnp.float32
            )
            * 0.125
        )
        d_values_all = jnp.einsum(
            "bgrqk,bqgrh->bkgh",
            probs.astype(jnp.bfloat16),
            d_heads_low,
            preferred_element_type=jnp.float32,
        )
        d_keys, d_values = (
            lax.psum_scatter(
                d_keys_all.astype(jnp.bfloat16), "ctx", scatter_dimension=1, tiled=True
            ).astype(jnp.float32),
            lax.psum_scatter(
                d_values_all.astype(jnp.bfloat16), "ctx", scatter_dimension=1, tiled=True
            ).astype(jnp.float32),
        )
        d_queries = rotate_back(d_queries.reshape(seq_micro, block_rows, HEADS, HEAD), cosine, sine)
        d_keys = rotate_back(d_keys, cosine, sine)
        d_mixed = jnp.concatenate(
            [
                d_queries.reshape(seq_micro, block_rows, D),
                d_keys.reshape(seq_micro, block_rows, kv_width),
                d_values.reshape(seq_micro, block_rows, kv_width),
            ],
            axis=-1,
        ).astype(jnp.bfloat16)
        d_normed = by_columns(d_mixed, w_attn[:, :qkv_cols])
        grad_attn = grad_attn + jnp.concatenate([over_rows(normed, d_mixed), grad_out_proj], axis=1)
        grad_gain_one = grad_gain_one + jnp.sum(d_normed * x_float * inv_one, axis=(0, 1))
        d_states = d_states + norm_back(d_normed, x_float, inv_one, gain_one)
        input_grads.append(d_states)

    def owner_layout(grad_whole):
        return grad_whole.reshape(
            D, dp_count, ctx_count, grad_whole.shape[1] // (dp_count * ctx_count)
        )

    by_ctx = (
        lax.all_to_all(
            owner_layout(grad_attn).astype(jnp.bfloat16),
            "ctx",
            split_axis=2,
            concat_axis=2,
            tiled=True,
        ).astype(jnp.float32),
        lax.all_to_all(
            owner_layout(grad_gu).astype(jnp.bfloat16),
            "ctx",
            split_axis=2,
            concat_axis=2,
            tiled=True,
        ).astype(jnp.float32),
        lax.all_to_all(
            owner_layout(grad_down).astype(jnp.bfloat16),
            "ctx",
            split_axis=2,
            concat_axis=2,
            tiled=True,
        ).astype(jnp.float32),
    )
    attn_ctx, gu_ctx, down_ctx = [jnp.sum(piece, axis=2) for piece in by_ctx]
    by_dp = (
        lax.all_to_all(shortened(attn_ctx), "dp", split_axis=1, concat_axis=1, tiled=True).astype(
            attn_ctx.dtype
        ),
        lax.all_to_all(shortened(gu_ctx), "dp", split_axis=1, concat_axis=1, tiled=True).astype(
            gu_ctx.dtype
        ),
        lax.all_to_all(shortened(down_ctx), "dp", split_axis=1, concat_axis=1, tiled=True).astype(
            down_ctx.dtype
        ),
    )
    attn_grad_part, gu_grad_part, down_grad_part = [jnp.sum(piece, axis=1) for piece in by_dp]
    grad_gains = jnp.stack([grad_gain_one, grad_gain_two], axis=0)
    energy_all, gains_all, router_all = lax.psum((energy, grad_gains, grad_router), ("dp", "ctx"))
    mse_loss = 2.0 * energy_all / (valid_total * D)
    return (
        jnp.concatenate(out_parts, axis=0),
        mse_loss,
        jnp.concatenate(input_grads, axis=0),
        attn_grad_part,
        gu_grad_part,
        down_grad_part,
        gains_all,
        router_all,
    )


def solution(mesh):
    placed = (
        P("dp", "ctx", None),
        P("dp", "ctx", None),
        P("dp", "ctx"),
        P("dp", "ctx"),
        P(None, ("dp", "ctx")),
        P(None, ("dp", "ctx")),
        P(None, ("dp", "ctx")),
        P(),
        P(),
    )
    return jax.shard_map(
        on_device,
        mesh=mesh,
        in_specs=placed,
        out_specs=(
            P("dp", "ctx", None),
            P(),
            P("dp", "ctx", None),
            P(None, ("dp", "ctx")),
            P(None, ("dp", "ctx")),
            P(None, ("dp", "ctx")),
            P(),
            P(),
        ),
        check_vma=False,
    )
```

profile of v0, /device:TPU:0, one launch (start us, length us, event | category | flops | bytes accessed | tf_op | source)
XLA Modules:
  0.0 1026.9 jit_solution(13568377429993740406)
XLA Ops:
  10.8 68.1 %all-gather.8.cloned.1.call-done = bf16[960,2560]{0,1:T(8,128)(2,1)} async-done(((bf16[960,80]{0,1:T(8,128)(2,1)}), bf16[960,2560]{0,1:T(8,128)(2,1)}) %all-gather.8.cloned.1.call-update) | async-done | bytes 4915216 | tf_op jit(solution)/shard_map/all_gather | solution.py:107
  110.5 15.0 %bitcast_reduce_fusion = (f32[2,5,3,256]{3,2,1,0:T(4,128)S(1)}, f32[2,5,1024,256,3]{3,2,4,1,0:T(8,128)}) fusion(bf16[2,256,5,3,32]{1,4,3,2,0:T(8,128)(2,1)S(1)} %bitcast.322, bf16[2,256,5,3,32]{1,4,3,2,0:T(8,128)(2,1)} %bitcast.324, bf16[2,1024,5,64]{1,3,2,0:T(8,128)(2,1)} %all-gather.20.cloned.1.call-done, pred[2,1024]{1,0:T(4,128)(4,1)S(1)} %get-tuple-element.98), kind=kOutput, calls=%fused_computation.12 | convolution fusion | flops 1032184320 | bytes 33783808 | tf_op jit(solution)/shard_map/bqgrh,bkgh->bgrqk/dot_general | solution.py:54
  125.5 13.0 %fusion.11 = f32[2,5,3,256]{3,2,1,0:T(4,128)S(1)} fusion(f32[2,5,1024,256,3]{3,2,4,1,0:T(8,128)} %get-tuple-element.100, f32[2,5,3,256]{3,2,1,0:T(4,128)S(1)} %get-tuple-element.99), kind=kLoop, calls=%fused_computation.25 | loop fusion | flops 15720960 | bytes 31518720 | tf_op jit(solution)/shard_map/reduce_sum | solution.py:134
  138.5 14.3 %bitcast_reduce_fusion.1 = (f32[2,5,3,256]{3,2,1,0:T(4,128)S(1)}, f32[2,5,1024,256,3]{3,2,4,1,0:T(8,128)}) fusion(bf16[2,256,5,3,32]{1,4,3,2,0:T(8,128)(2,1)S(1)} %bitcast.320, bf16[2,256,5,3,32]{1,4,3,2,0:T(8,128)(2,1)S(1)} %bitcast.318, bf16[2,1024,5,64]{1,3,2,0:T(8,128)(2,1)} %all-gather.12.cloned.1.call-done, pred[2,1024]{1,0:T(4,128)(4,1)S(1)} %get-tuple-element.97), kind=kOutput, calls=%fused_computation.17 | convolution fusion | flops 1032184320 | bytes 33783808 | tf_op jit(solution)/shard_map/bqgrh,bkgh->bgrqk/dot_general | solution.py:54
  152.8 13.1 %fusion.10 = f32[2,5,3,256]{3,2,1,0:T(4,128)S(1)} fusion(f32[2,5,1024,256,3]{3,2,4,1,0:T(8,128)} %get-tuple-element.102, f32[2,5,3,256]{3,2,1,0:T(4,128)S(1)} %get-tuple-element.101), kind=kLoop, calls=%fused_computation.24 | loop fusion | flops 15720960 | bytes 31518720 | tf_op jit(solution)/shard_map/reduce_sum | solution.py:134
  166.0 13.3 %fusion.72 = bf16[2,5,64,3,256]{4,2,3,1,0:T(8,128)(2,1)S(1)} fusion(f32[2,5,1024,256,3]{3,2,4,1,0:T(8,128)} %get-tuple-element.100, f32[2,5,3,256]{3,2,1,0:T(4,128)S(1)} %fusion.11, f32[2,5,3,256]{3,2,1,0:T(4,128)S(1)} %get-tuple-element.99, bf16[2,1024,5,64]{1,3,2,0:T(8,128)(2,1)} %all-gather.18.cloned.1.call-done), kind=kOutput, calls=%fused_computation.144 | convolution fusion | flops 1030717440 | bytes 33812480 | tf_op jit(solution)/shard_map/bgrqk,bkgh->bqgrh/dot_general | solution.py:137
  183.7 13.5 %fusion.73 = bf16[2,5,64,3,256]{4,2,3,1,0:T(8,128)(2,1)S(1)} fusion(f32[2,5,1024,256,3]{3,2,4,1,0:T(8,128)} %get-tuple-element.102, f32[2,5,3,256]{3,2,1,0:T(4,128)S(1)} %fusion.10, f32[2,5,3,256]{3,2,1,0:T(4,128)S(1)} %get-tuple-element.101, bf16[2,1024,5,64]{1,3,2,0:T(8,128)(2,1)} %all-gather.10.cloned.1.call-done), kind=kOutput, calls=%fused_computation.145 | convolution fusion | flops 1030717440 | bytes 33812480 | tf_op jit(solution)/shard_map/bgrqk,bkgh->bqgrh/dot_general | solution.py:137
  203.7 50.6 %all-gather.14.cloned.1.call-done = bf16[960,5120]{0,1:T(8,128)(2,1)} async-done(((bf16[960,160]{0,1:T(8,128)(2,1)}), bf16[960,5120]{0,1:T(8,128)(2,1)}) %all-gather.14.cloned.1.call-update) | async-done | bytes 9830416 | tf_op jit(solution)/shard_map/all_gather | solution.py:108
  284.5 36.5 %all-gather.16.cloned.1.call-done = bf16[960,2560]{0,1:T(8,128)(2,1)} async-done(((bf16[960,80]{0,1:T(8,128)(2,1)}), bf16[960,2560]{0,1:T(8,128)(2,1)}) %all-gather.16.cloned.1.call-update) | async-done | bytes 4915216 | tf_op jit(solution)/shard_map/all_gather | solution.py:109
  361.1 13.9 %fusion.25 = f32[2,256,960]{1,2,0:T(8,128)} fusion(bf16[960,5120]{0,1:T(8,128)(2,1)} %all-gather.14.cloned.1.call-done, bf16[2,256,2560]{2,1,0:T(8,128)(2,1)} %get-tuple-element.37, bf16[2,256,2560]{2,1,0:T(8,128)(2,1)S(1)} %get-tuple-element.36), kind=kOutput, calls=%fused_computation.38 | convolution fusion | flops 5043650560 | bytes 17039360 | tf_op jit(solution)/shard_map/dot_general | solution.py:66
  375.0 15.0 %multiply_reduce_fusion = (f32[960]{0:T(1024)}, f32[2,256]{1,0:T(2,128)S(1)}, f32[2,256]{1,0:T(2,128)S(1)}, f32[960]{0:T(1024)}, f32[2,256,960]{1,2,0:T(8,128)}) fusion(f32[2,256,960]{1,2,0:T(8,128)} %get-tuple-element.53, f32[2,256]{1,0:T(2,128)S(1)} %get-tuple-element.90, f32[960]{0:T(1024)S(1)} %bitcast.340, f32[2,256,960]{1,2,0:T(8,128)} %get-tuple-element.31, ...), kind=kOutput, calls=%fused_computation.116 | convolution fusion | flops 5049545728 | bytes 22957312 | tf_op jit(solution)/shard_map/dot_general | solution.py:66
  399.2 24.1 %fusion = (f32[2,5,3,256]{3,2,1,0:T(4,128)S(1)}, f32[2,5,1024,256,3]{3,2,4,1,0:T(8,128)}) fusion(f32[2,5,1024,256,3]{3,2,4,1,0:T(8,128)} %get-tuple-element.100, f32[2,5,3,256]{3,2,1,0:T(4,128)S(1)} %log_add_fusion, bf16[2,256,5,3,64]{1,4,3,2,0:T(8,128)(2,1)S(1)} %bitcast.312, bf16[2,1024,5,64]{1,3,2,0:T(8,128)(2,1)S(1)} %copy-done.26), kind=kOutput, calls=%fused_computation.2 | convolution fusion | flops 1030218240 | bytes 65269760 | tf_op jit(solution)/shard_map/bqgrh,bkgh->bgrqk/dot_general | solution.py:187
  423.3 26.8 %fusion.2 = bf16[2,5,3,256,1024]{3,4,2,1,0:T(8,128)(2,1)} fusion(f32[2,5,1024,256,3]{3,2,4,1,0:T(8,128)} %get-tuple-element.106, f32[2,5,1024,256,3]{3,2,4,1,0:T(8,128)} %get-tuple-element.100, f32[2,5,3,256]{3,2,1,0:T(4,128)S(1)} %get-tuple-element.105, f32[2,5,3,256]{3,2,1,0:T(4,128)S(1)} %log_add_fusion), kind=kLoop, calls=%fused_computation.4 | loop fusion | flops 31457280 | bytes 78704640 | tf_op jit(solution)/shard_map/convert_element_type | solution.py:190
  464.7 24.4 %fusion.3 = (f32[2,5,3,256]{3,2,1,0:T(4,128)S(1)}, f32[2,5,1024,256,3]{3,2,4,1,0:T(8,128)}) fusion(f32[2,5,1024,256,3]{3,2,4,1,0:T(8,128)} %get-tuple-element.102, f32[2,5,3,256]{3,2,1,0:T(4,128)S(1)} %copy-done.30, bf16[2,256,5,3,64]{1,4,3,2,0:T(8,128)(2,1)S(1)} %bitcast.310, bf16[2,1024,5,64]{1,3,2,0:T(8,128)(2,1)S(1)} %copy-done.25), kind=kOutput, calls=%fused_computation.7 | convolution fusion | flops 1030218240 | bytes 65269760 | tf_op jit(solution)/shard_map/bqgrh,bkgh->bgrqk/dot_general | solution.py:187
  489.1 26.6 %fusion.5 = bf16[2,5,3,256,1024]{3,4,2,1,0:T(8,128)(2,1)} fusion(f32[2,5,1024,256,3]{3,2,4,1,0:T(8,128)} %get-tuple-element.108, f32[2,5,1024,256,3]{3,2,4,1,0:T(8,128)} %get-tuple-element.102, f32[2,5,3,256]{3,2,1,0:T(4,128)S(1)} %get-tuple-element.107, f32[2,5,3,256]{3,2,1,0:T(4,128)S(1)} %copy-done.30), kind=kLoop, calls=%fused_computation.9 | loop fusion | flops 31457280 | bytes 78704640 | tf_op jit(solution)/shard_map/convert_element_type | solution.py:190
  527.3 14.8 %fusion.77 = bf16[2,1024,5,64]{1,3,2,0:T(8,128)(2,1)} fusion(bf16[2,256,5,3,64]{1,4,3,2,0:T(8,128)(2,1)} %bitcast.313, f32[2,5,1024,256,3]{3,2,4,1,0:T(8,128)} %get-tuple-element.100, f32[2,5,3,256]{3,2,1,0:T(4,128)S(1)} %log_add_fusion), kind=kOutput, calls=%fused_computation.147 | convolution fusion | flops 1023016960 | bytes 33781760 | tf_op jit(solution)/shard_map/bgrqk,bqgrh->bkgh/dot_general | solution.py:203
  570.1 14.1 %fusion.74 = bf16[2,1024,5,64]{1,3,2,0:T(8,128)(2,1)} fusion(bf16[2,256,5,3,64]{1,4,3,2,0:T(8,128)(2,1)S(1)} %bitcast.311, f32[2,5,1024,256,3]{3,2,4,1,0:T(8,128)} %get-tuple-element.102, f32[2,5,3,256]{3,2,1,0:T(4,128)S(1)} %copy-done.30), kind=kOutput, calls=%fused_computation.146 | convolution fusion | flops 1023016960 | bytes 33781760 | tf_op jit(solution)/shard_map/bgrqk,bqgrh->bkgh/dot_general | solution.py:203
  608.3 35.2 %all-to-all-done.4 = bf16[960,8,4,80]{0,3,1,2:T(8,128)(2,1)} async-done(((bf16[960,8,4,80]{0,3,1,2:T(8,128)(2,1)}), bf16[960,8,4,80]{0,3,1,2:T(8,128)(2,1)}, u32[]{:S(2)}, u32[]{:S(2)}) %all-to-all-start.4) | async-done | bytes 4915232 | tf_op jit(solution)/shard_map/all_to_all | solution.py:253
  700.1 12.3 %fusion.41 = f32[960,5120,1]{1,0,2:T(8,128)} fusion(bf16[2,256,2560]{2,1,0:T(8,128)(2,1)} %get-tuple-element.37, bf16[2,256,2560]{2,1,0:T(8,128)(2,1)} %copy-done.95, f32[2,256,960]{1,2,0:T(8,128)} %get-tuple-element.31, f32[960]{0:T(1024)S(1)} %bitcast.342, f32[2,256]{1,0:T(2,128)S(1)} %copy-done.56), kind=kOutput, calls=%fused_computation.84 | convolution fusion | flops 5045125120 | bytes 26875648 | tf_op jit(solution)/shard_map/dot_general | solution.py:60
  712.4 13.8 %fusion.14 = bf16[960,5120]{1,0:T(8,128)(2,1)} fusion(f32[960,5120,1]{1,0,2:T(8,128)} %fusion.41, bf16[2,256,2560]{2,1,0:T(8,128)(2,1)} %get-tuple-element.35, bf16[2,256,2560]{2,1,0:T(8,128)(2,1)} %get-tuple-element.34, f32[2,256,960]{1,2,0:T(8,128)} %get-tuple-element.53, f32[2,256]{1,0:T(2,128)S(1)} %copy-done.60, f32[960]{0:T(1024)S(1)} %bitcast.343), kind=kOutput, calls=%fused_computation.29 | convolution fusion | flops 5054955520 | bytes 36706048 | tf_op jit(solution)/shard_map/dot_general | solution.py:60
  726.1 14.2 %copy.57 = bf16[960,5120]{0,1:T(8,128)(2,1)} copy(bf16[960,5120]{1,0:T(8,128)(2,1)} %fusion.14) | data formatting | bytes 19660800 | tf_op jit(solution)/shard_map/convert_element_type | solution.py:247
  770.6 110.4 %all-to-all-done.2 = bf16[960,8,4,160]{0,3,1,2:T(8,128)(2,1)} async-done(((bf16[960,8,4,160]{0,3,1,2:T(8,128)(2,1)}), bf16[960,8,4,160]{0,3,1,2:T(8,128)(2,1)}, u32[]{:S(2)}, u32[]{:S(2)}) %all-to-all-start.2) | async-done | bytes 9830432 | tf_op jit(solution)/shard_map/all_to_all | solution.py:246
  897.2 21.3 %all-to-all-done.1 = bf16[960,8,80]{0,2,1:T(8,128)(2,1)} async-done(((bf16[960,8,80]{0,2,1:T(8,128)(2,1)}), bf16[960,8,80]{0,2,1:T(8,128)(2,1)}, u32[]{:S(2)}, u32[]{:S(2)}) %all-to-all-start.1) | async-done | bytes 1228832 | tf_op jit(solution)/shard_map/all_to_all | solution.py:263
  938.1 63.9 %all-reduce = (f32[]{:T(128)}, f32[]{:T(128)}, f32[2,960]{1,0:T(2,128)}, f32[960]{0:T(1024)}) all-reduce(f32[]{:T(128)S(6)} %add.239, f32[]{:T(128)} %convert_reduce_fusion.3, f32[2,960]{1,0:T(2,128)S(1)} %pad_maximum_fusion.26, f32[960]{0:T(1024)S(1)} %add.263), channel_id=1, replica_groups=mesh['dp'=8,'ctx'=4] {'dp','ctx'}, use_global_device_ids=true, to_apply=%region_10.11 | all-reduce | flops 2882 | bytes 23056 | tf_op jit(solution)/shard_map/psum | solution.py:275
  (333 shorter events, 339.7 us)
Async XLA Ops:
  7.2 71.7 %all-gather.8.cloned.1.call-start = ((), (), s32[]{:S(2)}) async-start(), calls=%async_computation.10 | async-start | bytes 5406720 | tf_op jit(solution)/shard_map/all_gather | solution.py:107
  7.9 102.6 %all-gather.20.cloned.1.call-start = ((), (), s32[]{:S(2)}) async-start(), calls=%async_computation.16 | async-start | bytes 1638400 | tf_op jit(solution)/shard_map/all_gather | solution.py:126
  10.5 379.4 %copy-start.44 = (f32[1,960]{1,0:T(1,128)}, f32[1,960]{1,0:T(1,128)S(1)}, u32[]{:S(2)}) copy-start(f32[1,960]{1,0:T(1,128)S(1)} %get-tuple-element.70) | copy-start | bytes 11524
  10.7 96.1 %copy-start.38 = (f32[256,32]{0,1:T(8,128)}, f32[256,32]{0,1:T(8,128)S(1)}, u32[]{:S(2)}) copy-start(f32[256,32]{0,1:T(8,128)S(1)} %get-tuple-element.95) | copy-start | bytes 98308
  87.7 50.7 %all-gather.12.cloned.1.call-start = ((), (), s32[]{:S(2)}) async-start(), calls=%async_computation.12 | async-start | bytes 1638400 | tf_op jit(solution)/shard_map/all_gather | solution.py:126
  88.5 77.4 %all-gather.18.cloned.1.call-start = ((), (), s32[]{:S(2)}) async-start(), calls=%async_computation.15 | async-start | bytes 1638400 | tf_op jit(solution)/shard_map/all_gather | solution.py:127
  90.5 93.2 %all-gather.10.cloned.1.call-start = ((), (), s32[]{:S(2)}) async-start(), calls=%async_computation.11 | async-start | bytes 1638400 | tf_op jit(solution)/shard_map/all_gather | solution.py:127
  92.4 161.9 %all-gather.14.cloned.1.call-start = ((), (), s32[]{:S(2)}) async-start(), calls=%async_computation.13 | async-start | bytes 10813440 | tf_op jit(solution)/shard_map/all_gather | solution.py:108
  93.0 228.0 %all-gather.16.cloned.1.call-start = ((), (), s32[]{:S(2)}) async-start(), calls=%async_computation.14 | async-start | bytes 5406720 | tf_op jit(solution)/shard_map/all_gather | solution.py:109
  93.7 564.2 %reduce-scatter.9.cloned.1.call-start = ((), (), s32[]{:S(2)}) async-start(), calls=%async_computation.19 | async-start | bytes 1638400 | tf_op jit(solution)/shard_map/reduce_scatter | solution.py:210
  203.0 187.0 %copy-start.53 = (f32[2,256]{1,0:T(2,128)}, f32[2,256]{1,0:T(2,128)S(1)}, u32[]{:S(2)}) copy-start(f32[2,256]{1,0:T(2,128)S(1)} %get-tuple-element.91) | copy-start | bytes 6148
  203.0 187.0 %copy-start.55 = (f32[2,256]{1,0:T(2,128)}, f32[2,256]{1,0:T(2,128)S(1)}, u32[]{:S(2)}) copy-start(f32[2,256]{1,0:T(2,128)S(1)} %get-tuple-element.92) | copy-start | bytes 6148
  203.0 187.0 %copy-start.57 = (f32[2,256]{1,0:T(2,128)}, f32[2,256]{1,0:T(2,128)S(1)}, u32[]{:S(2)}) copy-start(f32[2,256]{1,0:T(2,128)S(1)} %get-tuple-element.89) | copy-start | bytes 6148
  203.0 187.0 %copy-start.59 = (f32[2,256]{1,0:T(2,128)}, f32[2,256]{1,0:T(2,128)S(1)}, u32[]{:S(2)}) copy-start(f32[2,256]{1,0:T(2,128)S(1)} %get-tuple-element.90) | copy-start | bytes 6148
  461.5 198.3 %reduce-scatter.5.cloned.1.call-start = ((), (), s32[]{:S(2)}) async-start(), calls=%async_computation.17 | async-start | bytes 1638400 | tf_op jit(solution)/shard_map/reduce_scatter | solution.py:210
  527.3 136.5 %reduce-scatter.11.cloned.1.call-start = ((), (), s32[]{:S(2)}) async-start(), calls=%async_computation.20 | async-start | bytes 1638400 | tf_op jit(solution)/shard_map/reduce_scatter | solution.py:213
  564.9 78.5 %all-to-all-start.4 = ((bf16[960,8,4,80]{0,3,1,2:T(8,128)(2,1)}), bf16[960,8,4,80]{0,3,1,2:T(8,128)(2,1)}, u32[]{:S(2)}, u32[]{:S(2)}) async-start(bf16[960,8,4,80]{0,3,1,2:T(8,128)(2,1)} %copy.61), calls=%async_computation.8 | async-start | bytes 10485760 | tf_op jit(solution)/shard_map/all_to_all | solution.py:253
  570.0 99.9 %reduce-scatter.7.cloned.1.call-start = ((), (), s32[]{:S(2)}) async-start(), calls=%async_computation.18 | async-start | bytes 1638400 | tf_op jit(solution)/shard_map/reduce_scatter | solution.py:213
  648.7 46.1 %all-to-all-start.5 = ((bf16[960,8,80]{0,2,1:T(8,128)(2,1)}), bf16[960,8,80]{0,2,1:T(8,128)(2,1)S(1)}, u32[]{:S(2)}, u32[]{:S(2)}) async-start(bf16[960,8,80]{0,2,1:T(8,128)(2,1)} %reduce_sum.273), calls=%async_computation.9 | async-start | bytes 2621440 | tf_op jit(solution)/shard_map/all_to_all | solution.py:269
  694.8 64.7 %all-to-all-start = ((bf16[960,8,4,80]{0,3,1,2:T(8,128)(2,1)}), bf16[960,8,4,80]{0,3,1,2:T(8,128)(2,1)}, u32[]{:S(2)}, u32[]{:S(2)}) async-start(bf16[960,8,4,80]{0,3,1,2:T(8,128)(2,1)} %copy.55), calls=%async_computation.4 | async-start | bytes 10485760 | tf_op jit(solution)/shard_map/all_to_all | solution.py:239
  759.5 121.6 %all-to-all-start.2 = ((bf16[960,8,4,160]{0,3,1,2:T(8,128)(2,1)}), bf16[960,8,4,160]{0,3,1,2:T(8,128)(2,1)}, u32[]{:S(2)}, u32[]{:S(2)}) async-start(bf16[960,8,4,160]{0,3,1,2:T(8,128)(2,1)} %copy.58), calls=%async_computation.6 | async-start | bytes 20971520 | tf_op jit(solution)/shard_map/all_to_all | solution.py:246
  770.6 116.7 %copy-start.70 = (s32[4,256]{1,0:T(4,128)S(1)}, s32[4,256]{1,0:T(4,128)}, u32[]{:S(2)}) copy-start(s32[4,256]{1,0:T(4,128)} %param.11) | copy-start | bytes 12292
  881.0 37.4 %all-to-all-start.1 = ((bf16[960,8,80]{0,2,1:T(8,128)(2,1)}), bf16[960,8,80]{0,2,1:T(8,128)(2,1)}, u32[]{:S(2)}, u32[]{:S(2)}) async-start(bf16[960,8,80]{0,2,1:T(8,128)(2,1)} %reduce_sum.269), calls=%async_computation.5 | async-start | bytes 2621440 | tf_op jit(solution)/shard_map/all_to_all | solution.py:263
  918.4 97.5 %all-to-all-start.3 = ((bf16[960,8,160]{0,2,1:T(8,128)(2,1)}), bf16[960,8,160]{0,2,1:T(8,128)(2,1)}, u32[]{:S(2)}, u32[]{:S(2)}) async-start(bf16[960,8,160]{0,2,1:T(8,128)(2,1)} %reduce_sum.271), calls=%async_computation.7 | async-start | bytes 5242880 | tf_op jit(solution)/shard_map/all_to_all | solution.py:266
  (94 other events, 1399.9 us)
Sparse Core Ops, SparseCore 0:
  10.8 68.0 all-gather.7
  87.8 16.8 all-gather.19
  106.9 18.3 all-gather.11
  127.2 18.3 all-gather.17
  146.9 18.3 all-gather.9
  168.0 86.2 all-gather.13
  257.1 63.8 all-gather.15
  461.7 24.9 reduce-scatter.8
  527.4 24.9 reduce-scatter.4
  555.3 33.5 reduce-scatter.10
  591.5 33.5 reduce-scatter.6
where the time goes:
time: 1030 us
  matrix products  347 us (34%)
  waiting for transfers between devices  333 us (32%)
  other arithmetic  149 us (14%)
  blocking collectives  74.7 us (7%)
  local copies, waits for them, and re-layouts  71.1 us (7%)
  starting transfers between devices  31.9 us (3%)
  between operations  19.2 us (2%)
    all_to_all x1, waiting for transfers between devices, on_device(): lax.all_to_all(owner_layout(grad_gu).astype(jnp.bfloat16), 'ctx', split_a...  110 us
    all_gather x1, waiting for transfers between devices, on_device(): lax.all_gather(packs[0], ('dp', 'ctx'), axis=1, tiled=True)  68.1 us
    dot_general x8, matrix products, by_columns(): lax.dot_general(left, right, (((2,), (1,)), ((), ())), preferred_element_...  67.6 us
    psum x1, blocking collectives, on_device(): lax.psum((energy, grad_gains, grad_router), ('dp', 'ctx'))  63.9 us
    convert_element_type x2, other arithmetic, on_device(): (probs * (d_probs - jnp.sum(probs * d_probs, axis=-1, keepdims=True))).as...  53.3 us
    dot_general x8, matrix products, over_rows(): lax.dot_general(left, right, (((0, 1), (0, 1)), ((), ())), preferred_elem...  51 us
    all_gather x1, waiting for transfers between devices, on_device(): lax.all_gather(packs[1], ('dp', 'ctx'), axis=1, tiled=True)  50.6 us
    dot_general x2, matrix products, on_device(): jnp.einsum('bqgrh,bkgh->bgrqk', d_heads_low, values_all, preferred_elemen...  48.6 us
  transfers between devices with their start and end apart: 17, of which 7 were waited for; matrix products, arithmetic and copies ran while one was open for 39% of the time, Pallas kernels for 0%

commit v1 on v0

--- a/solution.py
+++ b/solution.py
@@ -11,6 +11,20 @@
 MICRO = 2
 EPS = 1e-05
 THETA = 10000.0
+
+
+def step_on_the_cards(u_in):
+    local_next, y = (lax.axis_size(("dp", "ctx")), lax.axis_index(("dp", "ctx")))
+    z_new, x_next = (u_in, 1)
+    while x_next < local_next:
+        mat_out = lax.ppermute(
+            z_new, ("dp", "ctx"), list(map(lambda h: (h, h ^ x_next), range(local_next)))
+        )
+        piece_next = jnp.concatenate([z_new, mat_out], 1)
+        f_next = jnp.concatenate([mat_out, z_new], 1)
+        z_new = jnp.where(y & x_next == 0, piece_next, f_next)
+        x_next = 2 * x_next
+    return z_new
 
 
 def shortened(x):
@@ -106,7 +120,7 @@
         fresh = (
             lax.all_gather(packs[0], ("dp", "ctx"), axis=1, tiled=True),
             lax.all_gather(packs[1], ("dp", "ctx"), axis=1, tiled=True),
-            lax.all_gather(packs[2], ("dp", "ctx"), axis=1, tiled=True),
+            step_on_the_cards(packs[2]),
         )
         w_attn, w_gu, w_down = fresh
         inv_one = lax.rsqrt(jnp.mean(x_float * x_float, axis=-1, keepdims=True) + EPS)

time: 1030 us -> 1120 us (1.087)
  waiting for transfers between devices: 333 us -> 403 us
  local copies, waits for them, and re-layouts: 71.1 us -> 86.8 us
    ppermute x0 -> x5, waiting for transfers between devices: none -> 157 us  [step_on_the_cards(): lax.ppermute(z_new, ('dp', 'ctx'), list(map(lambda h: (h, h ^ x_next), ra...]
    all_gather x1, waiting for transfers between devices: 50.6 us -> 0.01 us  [on_device(): lax.all_gather(packs[1], ('dp', 'ctx'), axis=1, tiled=True)]
    all_gather x1, waiting for transfers between devices: 36.5 us -> 0.01 us  [on_device(): lax.all_gather(packs[2], ('dp', 'ctx'), axis=1, tiled=True)]
  transfers between devices with their start and end apart: 17 -> 22, of which waited for: 7 -> 10; matrix products, arithmetic and copies ran while one was open for 39% -> 39% of each run, Pallas kernels for 0% -> 0%
where the time goes in v1:
time: 1120 us
  waiting for transfers between devices  403 us (36%)
  matrix products  337 us (30%)
  other arithmetic  156 us (14%)
  local copies, waits for them, and re-layouts  86.8 us (8%)
  blocking collectives  73.8 us (7%)
  starting transfers between devices  40.3 us (4%)
  between operations  19.2 us (2%)
    ppermute x5, waiting for transfers between devices, step_on_the_cards(): lax.ppermute(z_new, ('dp', 'ctx'), list(map(lambda h: (h, h ^ x_next), ra...  157 us
    all_to_all x1, waiting for transfers between devices, on_device(): lax.all_to_all(owner_layout(grad_gu).astype(jnp.bfloat16), 'ctx', split_a...  110 us
    all_gather x1, waiting for transfers between devices, on_device(): lax.all_gather(packs[0], ('dp', 'ctx'), axis=1, tiled=True)  66.3 us
    psum x1, blocking collectives, on_device(): lax.psum((energy, grad_gains, grad_router), ('dp', 'ctx'))  63.5 us
    dot_general x8, matrix products, by_columns(): lax.dot_general(left, right, (((2,), (1,)), ((), ())), preferred_element_...  61.8 us
    convert_element_type x2, other arithmetic, on_device(): (probs * (d_probs - jnp.sum(probs * d_probs, axis=-1, keepdims=True))).as...  53.4 us
    dot_general x8, matrix products, over_rows(): lax.dot_general(left, right, (((0, 1), (0, 1)), ((), ())), preferred_elem...  52.1 us
    dot_general x2, matrix products, on_device(): jnp.einsum('bqgrh,bkgh->bgrqk', d_heads_low, values_all, preferred_elemen...  49.1 us
  transfers between devices with their start and end apart: 22, of which 10 were waited for; matrix products, arithmetic and copies ran while one was open for 39% of the time, Pallas kernels for 0%

profile of v1, /device:TPU:0, one launch (start us, length us, event | category | flops | bytes accessed | tf_op | source)
XLA Modules:
  0.0 1116.0 jit_solution(15309844608433362363)
XLA Ops:
  12.6 66.3 %all-gather.8.cloned.1.call-done = bf16[960,2560]{0,1:T(8,128)(2,1)} async-done(((bf16[960,80]{0,1:T(8,128)(2,1)}), bf16[960,2560]{0,1:T(8,128)(2,1)}) %all-gather.8.cloned.1.call-update) | async-done | bytes 4915216 | tf_op jit(solution)/shard_map/all_gather | solution.py:121
  96.5 13.8 %collective-permute-done.1 = bf16[960,160]{0,1:T(8,128)(2,1)S(1)} collective-permute-done((bf16[960,160]{0,1:T(8,128)(2,1)S(1)}, bf16[960,160]{0,1:T(8,128)(2,1)S(1)}, u32[]{:S(2)}, u32[]{:S(2)}) %collective-permute-start.1) | collective-permute-done | bytes 307232 | tf_op jit(solution)/shard_map/ppermute | solution.py:20
  112.1 15.2 %collective-permute-done.2 = bf16[960,320]{0,1:T(8,128)(2,1)} collective-permute-done((bf16[960,320]{0,1:T(8,128)(2,1)S(1)}, bf16[960,320]{0,1:T(8,128)(2,1)}, u32[]{:S(2)}, u32[]{:S(2)}) %collective-permute-start.2) | collective-permute-done | bytes 614432 | tf_op jit(solution)/shard_map/ppermute | solution.py:20
  132.5 26.8 %collective-permute-done.3 = bf16[960,640]{1,0:T(8,128)(2,1)} collective-permute-done((bf16[960,640]{1,0:T(8,128)(2,1)}, bf16[960,640]{1,0:T(8,128)(2,1)}, u32[]{:S(2)}, u32[]{:S(2)}) %collective-permute-start.3) | collective-permute-done | bytes 1228832 | tf_op jit(solution)/shard_map/ppermute | solution.py:20
  184.8 99.3 %collective-permute-done.4 = bf16[960,1280]{1,0:T(8,128)(2,1)} collective-permute-done((bf16[960,1280]{1,0:T(8,128)(2,1)}, bf16[960,1280]{1,0:T(8,128)(2,1)}, u32[]{:S(2)}, u32[]{:S(2)}) %collective-permute-start.4) | collective-permute-done | bytes 2457632 | tf_op jit(solution)/shard_map/ppermute | solution.py:20
  292.5 14.9 %bitcast_reduce_fusion = (f32[2,5,3,256]{3,2,1,0:T(4,128)S(1)}, f32[2,5,1024,256,3]{3,2,4,1,0:T(8,128)}) fusion(bf16[2,256,5,3,32]{1,4,3,2,0:T(8,128)(2,1)S(1)} %bitcast.321, bf16[2,256,5,3,32]{1,4,3,2,0:T(8,128)(2,1)} %bitcast.323, bf16[2,1024,5,64]{1,3,2,0:T(8,128)(2,1)} %all-gather.18.cloned.1.call-done, pred[2,1024]{1,0:T(4,128)(4,1)S(1)} %get-tuple-element.98), kind=kOutput, calls=%fused_computation.12 | convolution fusion | flops 1032184320 | bytes 33783808 | tf_op jit(solution)/shard_map/bqgrh,bkgh->bgrqk/dot_general | solution.py:68
  307.4 13.5 %fusion.11 = f32[2,5,3,256]{3,2,1,0:T(4,128)S(1)} fusion(f32[2,5,1024,256,3]{3,2,4,1,0:T(8,128)} %get-tuple-element.100, f32[2,5,3,256]{3,2,1,0:T(4,128)S(1)} %get-tuple-element.99), kind=kLoop, calls=%fused_computation.25 | loop fusion | flops 15720960 | bytes 31518720 | tf_op jit(solution)/shard_map/reduce_sum | solution.py:148
  321.0 14.4 %bitcast_reduce_fusion.1 = (f32[2,5,3,256]{3,2,1,0:T(4,128)S(1)}, f32[2,5,1024,256,3]{3,2,4,1,0:T(8,128)}) fusion(bf16[2,256,5,3,32]{1,4,3,2,0:T(8,128)(2,1)S(1)} %bitcast.319, bf16[2,256,5,3,32]{1,4,3,2,0:T(8,128)(2,1)S(1)} %bitcast.317, bf16[2,1024,5,64]{1,3,2,0:T(8,128)(2,1)} %all-gather.12.cloned.1.call-done, pred[2,1024]{1,0:T(4,128)(4,1)S(1)} %get-tuple-element.97), kind=kOutput, calls=%fused_computation.17 | convolution fusion | flops 1032184320 | bytes 33783808 | tf_op jit(solution)/shard_map/bqgrh,bkgh->bgrqk/dot_general | solution.py:68
  335.4 13.1 %fusion.10 = f32[2,5,3,256]{3,2,1,0:T(4,128)S(1)} fusion(f32[2,5,1024,256,3]{3,2,4,1,0:T(8,128)} %get-tuple-element.102, f32[2,5,3,256]{3,2,1,0:T(4,128)S(1)} %get-tuple-element.101), kind=kLoop, calls=%fused_computation.24 | loop fusion | flops 15720960 | bytes 31518720 | tf_op jit(solution)/shard_map/reduce_sum | solution.py:148
  348.5 13.3 %fusion.73 = bf16[2,5,64,3,256]{4,2,3,1,0:T(8,128)(2,1)S(1)} fusion(f32[2,5,1024,256,3]{3,2,4,1,0:T(8,128)} %get-tuple-element.100, f32[2,5,3,256]{3,2,1,0:T(4,128)S(1)} %fusion.11, f32[2,5,3,256]{3,2,1,0:T(4,128)S(1)} %get-tuple-element.99, bf16[2,1024,5,64]{1,3,2,0:T(8,128)(2,1)} %all-gather.16.cloned.1.call-done), kind=kOutput, calls=%fused_computation.145 | convolution fusion | flops 1030717440 | bytes 33812480 | tf_op jit(solution)/shard_map/bgrqk,bkgh->bqgrh/dot_general | solution.py:151
  361.9 13.5 %fusion.74 = bf16[2,5,64,3,256]{4,2,3,1,0:T(8,128)(2,1)S(1)} fusion(f32[2,5,1024,256,3]{3,2,4,1,0:T(8,128)} %get-tuple-element.102, f32[2,5,3,256]{3,2,1,0:T(4,128)S(1)} %fusion.10, f32[2,5,3,256]{3,2,1,0:T(4,128)S(1)} %get-tuple-element.101, bf16[2,1024,5,64]{1,3,2,0:T(8,128)(2,1)} %all-gather.10.cloned.1.call-done), kind=kOutput, calls=%fused_computation.146 | convolution fusion | flops 1030717440 | bytes 33812480 | tf_op jit(solution)/shard_map/bgrqk,bkgh->bqgrh/dot_general | solution.py:151
  461.7 14.9 %multiply_reduce_fusion = (f32[960]{0:T(1024)}, f32[2,256]{1,0:T(2,128)S(1)}, f32[2,256]{1,0:T(2,128)S(1)}, f32[960]{0:T(1024)}, f32[2,256,960]{1,2,0:T(8,128)}) fusion(f32[2,256,960]{1,2,0:T(8,128)} %get-tuple-element.53, f32[2,256]{1,0:T(2,128)S(1)} %get-tuple-element.90, f32[960]{0:T(1024)S(1)} %bitcast.339, f32[2,256,960]{1,2,0:T(8,128)} %get-tuple-element.31, ...), kind=kOutput, calls=%fused_computation.117 | convolution fusion | flops 5049545728 | bytes 22957312 | tf_op jit(solution)/shard_map/dot_general | solution.py:80
  486.0 24.3 %fusion = (f32[2,5,3,256]{3,2,1,0:T(4,128)S(1)}, f32[2,5,1024,256,3]{3,2,4,1,0:T(8,128)}) fusion(f32[2,5,1024,256,3]{3,2,4,1,0:T(8,128)} %get-tuple-element.100, f32[2,5,3,256]{3,2,1,0:T(4,128)S(1)} %log_add_fusion, bf16[2,256,5,3,64]{1,4,3,2,0:T(8,128)(2,1)S(1)} %bitcast.311, bf16[2,1024,5,64]{1,3,2,0:T(8,128)(2,1)S(1)} %copy-done.28), kind=kOutput, calls=%fused_computation.2 | convolution fusion | flops 1030218240 | bytes 65269760 | tf_op jit(solution)/shard_map/bqgrh,bkgh->bgrqk/dot_general | solution.py:201
  510.3 26.8 %fusion.2 = bf16[2,5,3,256,1024]{3,4,2,1,0:T(8,128)(2,1)} fusion(f32[2,5,1024,256,3]{3,2,4,1,0:T(8,128)} %get-tuple-element.106, f32[2,5,1024,256,3]{3,2,4,1,0:T(8,128)} %get-tuple-element.100, f32[2,5,3,256]{3,2,1,0:T(4,128)S(1)} %get-tuple-element.105, f32[2,5,3,256]{3,2,1,0:T(4,128)S(1)} %log_add_fusion), kind=kLoop, calls=%fused_computation.4 | loop fusion | flops 31457280 | bytes 78704640 | tf_op jit(solution)/shard_map/convert_element_type | solution.py:204
  551.7 24.9 %fusion.3 = (f32[2,5,3,256]{3,2,1,0:T(4,128)S(1)}, f32[2,5,1024,256,3]{3,2,4,1,0:T(8,128)}) fusion(f32[2,5,1024,256,3]{3,2,4,1,0:T(8,128)} %get-tuple-element.102, f32[2,5,3,256]{3,2,1,0:T(4,128)S(1)} %copy-done.34, bf16[2,256,5,3,64]{1,4,3,2,0:T(8,128)(2,1)S(1)} %bitcast.309, bf16[2,1024,5,64]{1,3,2,0:T(8,128)(2,1)S(1)} %copy-done.27), kind=kOutput, calls=%fused_computation.7 | convolution fusion | flops 1030218240 | bytes 65269760 | tf_op jit(solution)/shard_map/bqgrh,bkgh->bgrqk/dot_general | solution.py:201
  576.5 26.6 %fusion.5 = bf16[2,5,3,256,1024]{3,4,2,1,0:T(8,128)(2,1)} fusion(f32[2,5,1024,256,3]{3,2,4,1,0:T(8,128)} %get-tuple-element.108, f32[2,5,1024,256,3]{3,2,4,1,0:T(8,128)} %get-tuple-element.102, f32[2,5,3,256]{3,2,1,0:T(4,128)S(1)} %get-tuple-element.107, f32[2,5,3,256]{3,2,1,0:T(4,128)S(1)} %copy-done.34), kind=kLoop, calls=%fused_computation.9 | loop fusion | flops 31457280 | bytes 78704640 | tf_op jit(solution)/shard_map/convert_element_type | solution.py:204
  614.7 14.5 %fusion.78 = bf16[2,1024,5,64]{1,3,2,0:T(8,128)(2,1)} fusion(bf16[2,256,5,3,64]{1,4,3,2,0:T(8,128)(2,1)} %bitcast.312, f32[2,5,1024,256,3]{3,2,4,1,0:T(8,128)} %get-tuple-element.100, f32[2,5,3,256]{3,2,1,0:T(4,128)S(1)} %log_add_fusion), kind=kOutput, calls=%fused_computation.148 | convolution fusion | flops 1023016960 | bytes 33781760 | tf_op jit(solution)/shard_map/bgrqk,bqgrh->bkgh/dot_general | solution.py:217
  657.1 14.4 %fusion.75 = bf16[2,1024,5,64]{1,3,2,0:T(8,128)(2,1)} fusion(bf16[2,256,5,3,64]{1,4,3,2,0:T(8,128)(2,1)S(1)} %bitcast.310, f32[2,5,1024,256,3]{3,2,4,1,0:T(8,128)} %get-tuple-element.102, f32[2,5,3,256]{3,2,1,0:T(4,128)S(1)} %copy-done.34), kind=kOutput, calls=%fused_computation.147 | convolution fusion | flops 1023016960 | bytes 33781760 | tf_op jit(solution)/shard_map/bgrqk,bqgrh->bkgh/dot_general | solution.py:217
  693.0 37.5 %all-to-all-done.4 = bf16[960,8,4,80]{0,3,1,2:T(8,128)(2,1)} async-done(((bf16[960,8,4,80]{0,3,1,2:T(8,128)(2,1)}), bf16[960,8,4,80]{0,3,1,2:T(8,128)(2,1)}, u32[]{:S(2)}, u32[]{:S(2)}) %all-to-all-start.4) | async-done | bytes 4915232 | tf_op jit(solution)/shard_map/all_to_all | solution.py:267
  801.2 13.7 %fusion.14 = bf16[960,5120]{1,0:T(8,128)(2,1)} fusion(f32[960,5120,1]{1,0,2:T(8,128)} %fusion.38, bf16[2,256,2560]{2,1,0:T(8,128)(2,1)} %get-tuple-element.35, bf16[2,256,2560]{2,1,0:T(8,128)(2,1)} %get-tuple-element.34, f32[2,256,960]{1,2,0:T(8,128)} %get-tuple-element.53, f32[2,256]{1,0:T(2,128)S(1)} %copy-done.63, f32[960]{0:T(1024)S(1)} %bitcast.342), kind=kOutput, calls=%fused_computation.29 | convolution fusion | flops 5054955520 | bytes 36706048 | tf_op jit(solution)/shard_map/dot_general | solution.py:74
  814.9 14.3 %copy.93 = bf16[960,5120]{0,1:T(8,128)(2,1)} copy(bf16[960,5120]{1,0:T(8,128)(2,1)} %fusion.14) | data formatting | bytes 19660800 | tf_op jit(solution)/shard_map/convert_element_type | solution.py:261
  859.5 110.4 %all-to-all-done.2 = bf16[960,8,4,160]{0,3,1,2:T(8,128)(2,1)} async-done(((bf16[960,8,4,160]{0,3,1,2:T(8,128)(2,1)}), bf16[960,8,4,160]{0,3,1,2:T(8,128)(2,1)}, u32[]{:S(2)}, u32[]{:S(2)}) %all-to-all-start.2) | async-done | bytes 9830432 | tf_op jit(solution)/shard_map/all_to_all | solution.py:260
  986.3 21.2 %all-to-all-done.1 = bf16[960,8,80]{0,2,1:T(8,128)(2,1)} async-done(((bf16[960,8,80]{0,2,1:T(8,128)(2,1)}), bf16[960,8,80]{0,2,1:T(8,128)(2,1)}, u32[]{:S(2)}, u32[]{:S(2)}) %all-to-all-start.1) | async-done | bytes 1228832 | tf_op jit(solution)/shard_map/all_to_all | solution.py:277
  1027.5 63.5 %all-reduce = (f32[]{:T(128)}, f32[]{:T(128)}, f32[2,960]{1,0:T(2,128)}, f32[960]{0:T(1024)}) all-reduce(f32[]{:T(128)S(6)} %add.244, f32[]{:T(128)} %convert_reduce_fusion.3, f32[2,960]{1,0:T(2,128)S(1)} %pad_maximum_fusion.26, f32[960]{0:T(1024)S(1)} %add.268), channel_id=1, replica_groups=mesh['dp'=8,'ctx'=4] {'dp','ctx'}, use_global_device_ids=true, to_apply=%region_10.11 | all-reduce | flops 2882 | bytes 23056 | tf_op jit(solution)/shard_map/psum | solution.py:289
  (348 shorter events, 385.6 us)
Async XLA Ops:
  7.2 71.7 %all-gather.8.cloned.1.call-start = ((), (), s32[]{:S(2)}) async-start(), calls=%async_computation.10 | async-start | bytes 5406720 | tf_op jit(solution)/shard_map/all_gather | solution.py:121
  7.9 284.6 %all-gather.18.cloned.1.call-start = ((), (), s32[]{:S(2)}) async-start(), calls=%async_computation.15 | async-start | bytes 1638400 | tf_op jit(solution)/shard_map/all_gather | solution.py:140
  12.6 276.0 %copy-start.41 = (f32[256,32]{0,1:T(8,128)}, f32[256,32]{0,1:T(8,128)S(1)}, u32[]{:S(2)}) copy-start(f32[256,32]{0,1:T(8,128)S(1)} %get-tuple-element.95) | copy-start | bytes 98308
  12.6 276.0 %copy-start.43 = (f32[256,32]{0,1:T(8,128)}, f32[256,32]{0,1:T(8,128)S(1)}, u32[]{:S(2)}) copy-start(f32[256,32]{0,1:T(8,128)S(1)} %get-tuple-element.96) | copy-start | bytes 98308
  88.0 233.0 %all-gather.12.cloned.1.call-start = ((), (), s32[]{:S(2)}) async-start(), calls=%async_computation.12 | async-start | bytes 1638400 | tf_op jit(solution)/shard_map/all_gather | solution.py:140
  88.8 259.7 %all-gather.16.cloned.1.call-start = ((), (), s32[]{:S(2)}) async-start(), calls=%async_computation.14 | async-start | bytes 1638400 | tf_op jit(solution)/shard_map/all_gather | solution.py:141
  90.7 271.1 %all-gather.10.cloned.1.call-start = ((), (), s32[]{:S(2)}) async-start(), calls=%async_computation.11 | async-start | bytes 1638400 | tf_op jit(solution)/shard_map/all_gather | solution.py:141
  92.7 292.8 %all-gather.14.cloned.1.call-start = ((), (), s32[]{:S(2)}) async-start(), calls=%async_computation.13 | async-start | bytes 10813440 | tf_op jit(solution)/shard_map/all_gather | solution.py:122
  93.2 338.4 %all-gather.20.cloned.1.call-start = ((), (), s32[]{:S(2)}) async-start(), calls=%async_computation.16 | async-start | bytes 5406720 | tf_op jit(solution)/shard_map/all_gather | solution.py:175
  93.3 1.7 collective-permute-start
  95.1 15.3 %collective-permute-start.1 = (bf16[960,160]{0,1:T(8,128)(2,1)S(1)}, bf16[960,160]{0,1:T(8,128)(2,1)S(1)}, u32[]{:S(2)}, u32[]{:S(2)}) collective-permute-start(bf16[960,160]{0,1:T(8,128)(2,1)S(1)} %maximum_select_fusion.4), channel_id=1, source_target_pairs={{0,2},{1,3},{2,0},{3,1},{4,6},{5,7},{6,4},{7,5},{8,10},{9,11},{10,... | collective-permute-start | bytes 921608 | tf_op jit(solution)/shard_map/ppermute | solution.py:20
  110.6 16.7 %collective-permute-start.2 = (bf16[960,320]{0,1:T(8,128)(2,1)S(1)}, bf16[960,320]{0,1:T(8,128)(2,1)}, u32[]{:S(2)}, u32[]{:S(2)}) collective-permute-start(bf16[960,320]{0,1:T(8,128)(2,1)S(1)} %maximum_select_fusion.3), channel_id=1, source_target_pairs={{0,4},{1,5},{2,6},{3,7},{4,0},{5,1},{6,2},{7,3},{8,12},{9,13},{10,... | collective-permute-start | bytes 1843208 | tf_op jit(solution)/shard_map/ppermute | solution.py:20
  131.0 28.3 %collective-permute-start.3 = (bf16[960,640]{1,0:T(8,128)(2,1)}, bf16[960,640]{1,0:T(8,128)(2,1)}, u32[]{:S(2)}, u32[]{:S(2)}) collective-permute-start(bf16[960,640]{1,0:T(8,128)(2,1)} %copy.73), channel_id=1, source_target_pairs={{0,8},{1,9},{2,10},{3,11},{4,12},{5,13},{6,14},{7,15},{8,0},{9,1},... | collective-permute-start | bytes 3686408 | tf_op jit(solution)/shard_map/ppermute | solution.py:20
  169.9 114.3 %collective-permute-start.4 = (bf16[960,1280]{1,0:T(8,128)(2,1)}, bf16[960,1280]{1,0:T(8,128)(2,1)}, u32[]{:S(2)}, u32[]{:S(2)}) collective-permute-start(bf16[960,1280]{1,0:T(8,128)(2,1)} %copy.76), channel_id=1, source_target_pairs={{0,16},{1,17},{2,18},{3,19},{4,20},{5,21},{6,22},{7,23},{8,24},{9,... | collective-permute-start | bytes 7372808 | tf_op jit(solution)/shard_map/ppermute | solution.py:20
  172.2 574.4 %reduce-scatter.9.cloned.1.call-start = ((), (), s32[]{:S(2)}) async-start(), calls=%async_computation.19 | async-start | bytes 1638400 | tf_op jit(solution)/shard_map/reduce_scatter | solution.py:224
  548.5 200.1 %reduce-scatter.5.cloned.1.call-start = ((), (), s32[]{:S(2)}) async-start(), calls=%async_computation.17 | async-start | bytes 1638400 | tf_op jit(solution)/shard_map/reduce_scatter | solution.py:224
  614.7 137.8 %reduce-scatter.11.cloned.1.call-start = ((), (), s32[]{:S(2)}) async-start(), calls=%async_computation.20 | async-start | bytes 1638400 | tf_op jit(solution)/shard_map/reduce_scatter | solution.py:227
  651.9 78.5 %all-to-all-start.4 = ((bf16[960,8,4,80]{0,3,1,2:T(8,128)(2,1)}), bf16[960,8,4,80]{0,3,1,2:T(8,128)(2,1)}, u32[]{:S(2)}, u32[]{:S(2)}) async-start(bf16[960,8,4,80]{0,3,1,2:T(8,128)(2,1)} %copy.97), calls=%async_computation.8 | async-start | bytes 10485760 | tf_op jit(solution)/shard_map/all_to_all | solution.py:267
  657.0 101.5 %reduce-scatter.7.cloned.1.call-start = ((), (), s32[]{:S(2)}) async-start(), calls=%async_computation.18 | async-start | bytes 1638400 | tf_op jit(solution)/shard_map/reduce_scatter | solution.py:227
  735.7 47.8 %all-to-all-start.5 = ((bf16[960,8,80]{0,2,1:T(8,128)(2,1)}), bf16[960,8,80]{0,2,1:T(8,128)(2,1)S(1)}, u32[]{:S(2)}, u32[]{:S(2)}) async-start(bf16[960,8,80]{0,2,1:T(8,128)(2,1)} %reduce_sum.273), calls=%async_computation.9 | async-start | bytes 2621440 | tf_op jit(solution)/shard_map/all_to_all | solution.py:283
  783.5 64.8 %all-to-all-start = ((bf16[960,8,4,80]{0,3,1,2:T(8,128)(2,1)}), bf16[960,8,4,80]{0,3,1,2:T(8,128)(2,1)}, u32[]{:S(2)}, u32[]{:S(2)}) async-start(bf16[960,8,4,80]{0,3,1,2:T(8,128)(2,1)} %copy.91), calls=%async_computation.4 | async-start | bytes 10485760 | tf_op jit(solution)/shard_map/all_to_all | solution.py:253
  848.3 121.6 %all-to-all-start.2 = ((bf16[960,8,4,160]{0,3,1,2:T(8,128)(2,1)}), bf16[960,8,4,160]{0,3,1,2:T(8,128)(2,1)}, u32[]{:S(2)}, u32[]{:S(2)}) async-start(bf16[960,8,4,160]{0,3,1,2:T(8,128)(2,1)} %copy.94), calls=%async_computation.6 | async-start | bytes 20971520 | tf_op jit(solution)/shard_map/all_to_all | solution.py:260
  969.9 37.6 %all-to-all-start.1 = ((bf16[960,8,80]{0,2,1:T(8,128)(2,1)}), bf16[960,8,80]{0,2,1:T(8,128)(2,1)}, u32[]{:S(2)}, u32[]{:S(2)}) async-start(bf16[960,8,80]{0,2,1:T(8,128)(2,1)} %reduce_sum.269), calls=%async_computation.5 | async-start | bytes 2621440 | tf_op jit(solution)/shard_map/all_to_all | solution.py:277
  1007.5 97.4 %all-to-all-start.3 = ((bf16[960,8,160]{0,2,1:T(8,128)(2,1)}), bf16[960,8,160]{0,2,1:T(8,128)(2,1)}, u32[]{:S(2)}, u32[]{:S(2)}) async-start(bf16[960,8,160]{0,2,1:T(8,128)(2,1)} %reduce_sum.271), calls=%async_computation.7 | async-start | bytes 5242880 | tf_op jit(solution)/shard_map/all_to_all | solution.py:280
  (98 other events, 2074.6 us)
Sparse Core Ops, SparseCore 0:
  10.8 68.0 all-gather.7
  88.1 22.1 all-gather.17
  111.9 19.8 all-gather.11
  133.8 18.3 all-gather.15
  153.5 18.3 all-gather.9
  174.6 174.1 all-gather.13
  351.7 63.8 all-gather.19
  548.6 26.4 reduce-scatter.8
  614.8 26.5 reduce-scatter.4
  644.3 33.5 reduce-scatter.10
  680.5 33.6 reduce-scatter.6
